TPU v7x, 32 devices: a whole 2x2x4 slice. The times are simulated.
32 devices in a mesh: teacher: 4 (over y, x), vocab: 8 (over z, core).
Axes of the slice: x: 2, y: 2, z: 4, core: 2. Of those that a mesh axis runs over, the one named last changes fastest.
Arguments:
- teacher_hidden: bfloat16 [4, 1024, 4096], P('teacher', 'vocab'), may hold values from -180 to 180
- teacher_head: bfloat16 [4, 4096, 32000], P('teacher', None, 'vocab'), may hold values from -0.375 to 0.375
- student_hidden: bfloat16 [1024, 4096], P('teacher'), may hold values from -180 to 180
- student_head: bfloat16 [4096, 32000], P('teacher', 'vocab'), may hold values from -0.375 to 0.375
Outputs:
- loss: float32 [], replicated
- grad_hidden: float32 [1024, 4096], P('teacher', 'vocab')
- grad_weight: float32 [4096, 32000], P('teacher', 'vocab')
All inputs are finite; a program needn't handle non-finite values.
Results may differ from a plain program's by a relative error of at most 0.0027.
Values may be sent and summed in bfloat16 or wider, within the bound.
A program may use at most 192 MiB of HBM per device.

v0:
```python
import jax
import jax.numpy as jnp
from jax import lax
from jax.sharding import PartitionSpec as P

TOK = 1024


def teacher_stats(logits):
    local_top = jnp.max(logits, axis=-1)
    top = lax.pmax(local_top, "vocab")
    shifted = jnp.exp(logits - top[:, None])
    total, moment = lax.psum(
        (jnp.sum(shifted, axis=-1), jnp.sum(shifted * logits, axis=-1)), "vocab"
    )
    return (top, total, moment)


def paired_lse(stacked):
    local_top = jnp.max(stacked, axis=-1)
    top = lax.pmax(local_top, "vocab")
    total = lax.psum(jnp.sum(jnp.exp(stacked - top[..., None]), axis=-1), "vocab")
    return top + jnp.log(total)


def per_device(teacher_hidden, teacher_head, student_hidden, student_head):
    head = teacher_head[0]
    logits = jnp.dot(
        lax.all_gather(teacher_hidden[0], "vocab", axis=0, tiled=True),
        head,
        preferred_element_type=jnp.float32,
    )
    top, total, moment = teacher_stats(logits)
    lse = top + jnp.log(total)
    entropy = lse - moment / total
    confid = jnp.exp(-entropy)
    weighted = confid[:, None] * (logits - lse[:, None])
    wsum, csum = (
        lax.psum_scatter(weighted, "teacher", scatter_dimension=0, tiled=True),
        lax.psum_scatter(confid, "teacher", scatter_dimension=0, tiled=True),
    )
    raw = wsum / csum[:, None]
    full_head = lax.all_gather(student_head, "teacher", axis=0, tiled=True)
    slog = jnp.dot(student_hidden, full_head, preferred_element_type=jnp.float32)
    both_lse = paired_lse(jnp.stack([raw, slog]))
    target = raw - both_lse[0][:, None]
    slp = slog - both_lse[1][:, None]
    probs = jnp.exp(target)
    partial_kl = jnp.sum(probs * (target - slp))
    loss = lax.psum(partial_kl, ("teacher", "vocab")) / TOK
    gradl = (jnp.exp(slp) - probs).astype(jnp.bfloat16)
    grad_hidden = lax.psum_scatter(
        lax.dot_general(
            full_head, gradl, (((1,), (1,)), ((), ())), preferred_element_type=jnp.float32
        ),
        "vocab",
        scatter_dimension=0,
        tiled=True,
    ).T
    columns = lax.all_to_all(student_hidden, "teacher", split_axis=1, concat_axis=0, tiled=True)
    all_grads = lax.all_gather(gradl, "teacher", axis=0, tiled=True)
    grad_weight = lax.dot_general(
        columns, all_grads, (((0,), (0,)), ((), ())), preferred_element_type=jnp.float32
    )
    return (loss, grad_hidden, grad_weight)


def solution(mesh):
    placed = (
        P("teacher", "vocab", None),
        P("teacher", None, "vocab"),
        P("teacher", None),
        P("teacher", "vocab"),
    )
    return jax.shard_map(
        per_device,
        mesh=mesh,
        in_specs=placed,
        out_specs=(P(), P("teacher", "vocab"), P("teacher", "vocab")),
        check_vma=False,
    )
```

profile of v0, /device:TPU:0, one launch (start us, length us, event | category | flops | bytes accessed | tf_op | source)
XLA Modules:
  0.0 849.6 jit_solution(5529223192047300215)
XLA Ops:
  7.2 0.7 all-gather.9.cloned.1.call-update
  7.9 0.0 reduce-scatter.3.cloned.1.call-start
  7.9 86.4 %all-gather.9.cloned.1.call-done = bf16[1,1024,4096]{2,1,0:T(8,128)(2,1)} async-done(((bf16[1,128,4096]{2,1,0:T(8,128)(2,1)}), bf16[1,1024,4096]{2,1,0:T(8,128)(2,1)}) %all-gather.9.cloned.1.call-update) | async-done | bytes 8388624 | tf_op jit(solution)/shard_map/all_gather | solution.py:29
  94.4 41.8 %fusion.7 = (f32[1024]{0:T(1024)S(1)}, f32[1024,4000]{0,1:T(8,128)}) fusion(bf16[1,4096,4000]{1,2,0:T(8,128)(2,1)} %param.5, bf16[1,1024,4096]{2,1,0:T(8,128)(2,1)} %all-gather.9.cloned.1.call-done), kind=kOutput, calls=%fused_computation.20 | convolution fusion | flops 33558528000 | bytes 57544704 | tf_op jit(solution)/shard_map/dot_general | solution.py:28
  136.2 14.0 %pmax.14 = f32[1024]{0:T(1024)S(1)} all-reduce(f32[1024]{0:T(1024)S(1)} %get-tuple-element.13), channel_id=1, replica_groups=mesh['teacher'=4,'vocab'=8] {'vocab'}, use_global_device_ids=true, to_apply=%region_1.0 | all-reduce | flops 1024 | bytes 8192 | tf_op jit(solution)/shard_map/pmax | solution.py:11
  150.2 7.6 multiply_reduce_fusion
  157.8 13.9 %all-reduce.1 = (f32[1024]{0:T(1024)S(1)}, f32[1024]{0:T(1024)S(1)}) all-reduce(f32[1024]{0:T(1024)S(1)} %get-tuple-element.4, f32[1024]{0:T(1024)S(1)} %get-tuple-element.3), channel_id=1, replica_groups=mesh['teacher'=4,'vocab'=8] {'vocab'}, use_global_device_ids=true, to_apply=%region_3.0 | all-reduce | flops 2048 | bytes 16384 | tf_op jit(solution)/shard_map/psum | solution.py:13
  171.7 11.5 %subtract_multiply_fusion = f32[1024,4000]{0,1:T(8,128)} fusion(f32[1024,4000]{0,1:T(8,128)} %get-tuple-element.14, f32[1024]{0:T(1024)S(1)} %get-tuple-element.10, f32[1024]{0:T(1024)S(1)} %get-tuple-element.9), kind=kLoop, calls=%fused_computation.2 | loop fusion | flops 8192000 | bytes 32776192 | tf_op jit(solution)/shard_map/mul | solution.py:37
  183.3 0.0 all-gather.5.cloned.1.call-start
  183.3 0.7 all-gather.5.cloned.1.call-update
  184.1 0.6 dynamic-slice
  185.3 10.4 %all-reduce = f32[1024]{0:T(1024)S(1)} all-reduce(f32[1024]{0:T(1024)S(1)} %get-tuple-element.9), channel_id=4, replica_groups=mesh['teacher'=4,'vocab'=8] {'teacher'}, use_global_device_ids=true, to_apply=%region_7.0.clone | all-reduce | flops 1024 | bytes 8192
  195.7 0.1 dynamic-slice.1
  195.8 136.6 %reduce-scatter.3.cloned.1.call-done = f32[256,4000]{0,1:T(8,128)} async-done(((f32[1024,4000]{0,1:T(8,128)}), f32[256,4000]{0,1:T(8,128)}) %reduce-scatter.3.cloned.1.call-update) | async-done | bytes 4096016 | tf_op jit(solution)/shard_map/reduce_scatter | solution.py:39
  332.4 4.4 fusion.5
  336.8 288.4 %all-gather.5.cloned.1.call-done = bf16[4096,4000]{0,1:T(8,128)(2,1)} async-done(((bf16[1024,4000]{0,1:T(8,128)(2,1)}), bf16[4096,4000]{0,1:T(8,128)(2,1)}) %all-gather.5.cloned.1.call-update) | async-done | bytes 32768016 | tf_op jit(solution)/shard_map/all_gather | solution.py:43
  625.1 14.1 %fusion.8 = f32[256,4000]{0,1:T(8,128)S(1)} fusion(bf16[256,4096]{1,0:T(8,128)(2,1)S(1)} %copy-done.2, bf16[4096,4000]{0,1:T(8,128)(2,1)} %all-gather.5.cloned.1.call-done), kind=kOutput, calls=%fused_computation.21 | convolution fusion | flops 8388608000 | bytes 38961152 | tf_op jit(solution)/shard_map/dot_general | solution.py:44
  639.3 2.0 copy-done.1
  641.2 0.6 fusion.4
  641.8 16.3 %pmax.15 = f32[2,256]{1,0:T(2,128)S(1)} all-reduce(f32[2,256]{1,0:T(2,128)S(1)} %fusion.4), channel_id=1, replica_groups=mesh['teacher'=4,'vocab'=8] {'vocab'}, use_global_device_ids=true, to_apply=%region_9.0 | all-reduce | flops 512 | bytes 4096 | tf_op jit(solution)/shard_map/pmax | solution.py:21
  658.2 4.0 exponential_reduce_fusion
  662.1 13.8 %psum.30 = f32[2,256]{1,0:T(2,128)S(1)} all-reduce(f32[2,256]{1,0:T(2,128)S(1)} %exponential_reduce_fusion), channel_id=1, replica_groups=mesh['teacher'=4,'vocab'=8] {'vocab'}, use_global_device_ids=true, to_apply=%region_11.0 | all-reduce | flops 512 | bytes 4096 | tf_op jit(solution)/shard_map/psum | solution.py:22
  675.9 6.9 subtract_convert_fusion
  682.9 0.0 reduce-scatter.5.cloned.1.call-start
  682.9 18.8 %convolution_bitcast_fusion.1 = f32[4096,256]{0,1:T(8,128)} fusion(bf16[256,4000]{0,1:T(8,128)(2,1)} %get-tuple-element.7, bf16[4096,4000]{0,1:T(8,128)(2,1)} %all-gather.5.cloned.1.call-done), kind=kOutput, calls=%fused_computation.11 | convolution fusion | flops 8388608000 | bytes 39010304 | tf_op jit(solution)/shard_map/dot_general | solution.py:53
  701.8 2.5 copy.9
  704.2 32.7 %all_to_all.19 = bf16[256,4,1024]{0,2,1:T(8,128)(2,1)S(1)} all-to-all(bf16[256,4,1024]{0,2,1:T(8,128)(2,1)} %bitcast.33), channel_id=1, replica_groups=mesh['teacher'=4,'vocab'=8] {'teacher'}, dimensions={1} | all-to-all | bytes 4194304 | tf_op jit(solution)/shard_map/all_to_all | solution.py:60
  736.9 2.5 copy.10
  739.4 40.0 %psum.31 = f32[]{:T(128)} all-reduce(f32[]{:T(128)} %get-tuple-element.8), channel_id=1, replica_groups=mesh['teacher'=4,'vocab'=8] {'teacher','vocab'}, use_global_device_ids=true, to_apply=%region_13.0 | all-reduce | flops 1 | bytes 8 | tf_op jit(solution)/shard_map/psum | solution.py:50
  780.0 9.0 %all-gather.7.cloned.1.call-done = bf16[1024,4000]{0,1:T(8,128)(2,1)} async-done(((bf16[256,4000]{0,1:T(8,128)(2,1)}), bf16[1024,4000]{0,1:T(8,128)(2,1)}) %all-gather.7.cloned.1.call-update) | async-done | bytes 8192016 | tf_op jit(solution)/shard_map/all_gather | solution.py:61
  789.1 15.9 %convolution_bitcast_fusion = f32[1024,4000]{0,1:T(8,128)} fusion(bf16[1024,4000]{0,1:T(8,128)(2,1)} %all-gather.7.cloned.1.call-done, bf16[1024,1024]{1,0:T(8,128)(2,1)} %bitcast.34), kind=kOutput, calls=%fused_computation.6 | convolution fusion | flops 8388608000 | bytes 26673152 | tf_op jit(solution)/shard_map/dot_general | solution.py:62
  804.9 37.0 %reduce-scatter.5.cloned.1.call-done = f32[512,256]{0,1:T(8,128)} async-done(((f32[4096,256]{0,1:T(8,128)}), f32[512,256]{0,1:T(8,128)}) %reduce-scatter.5.cloned.1.call-update) | async-done | bytes 524304 | tf_op jit(solution)/shard_map/reduce_scatter | solution.py:52
  (15 shorter events, 0.2 us)
Async XLA Ops:
  7.2 87.2 %all-gather.9.cloned.1.call-start = ((), (), s32[]{:S(2)}) async-start(), calls=%async_computation.7 | async-start | bytes 9437184 | tf_op jit(solution)/shard_map/all_gather | solution.py:29
  7.9 324.5 %reduce-scatter.3.cloned.1.call-start = ((), (), s32[]{:S(2)}) async-start(), calls=%async_computation.3 | async-start | bytes 20480000 | tf_op jit(solution)/shard_map/reduce_scatter | solution.py:39
  183.3 0.8 copy-start.3
  183.3 441.8 %copy-start.2 = (bf16[256,4096]{1,0:T(8,128)(2,1)S(1)}, bf16[256,4096]{1,0:T(8,128)(2,1)}, u32[]{:S(2)}) copy-start(bf16[256,4096]{1,0:T(8,128)(2,1)} %param.6) | copy-start | bytes 6291460
  183.3 441.8 %all-gather.5.cloned.1.call-start = ((), (), s32[]{:S(2)}) async-start(), calls=%async_computation.4 | async-start | bytes 40960000 | tf_op jit(solution)/shard_map/all_gather | solution.py:43
  184.0 605.0 %all-gather.7.cloned.1.call-start = ((), (), s32[]{:S(2)}) async-start(), calls=%async_computation.6 | async-start | bytes 10240000 | tf_op jit(solution)/shard_map/all_gather | solution.py:61
  625.1 16.1 %copy-start = (f32[1,256,4000]{1,2,0:T(8,128)S(1)}, f32[1,256,4000]{1,2,0:T(8,128)}, u32[]{:S(2)}) copy-start(f32[1,256,4000]{1,2,0:T(8,128)} %fusion.5) | copy-start | bytes 12288004
  639.3 2.0 copy-start.1
  682.9 159.0 %reduce-scatter.5.cloned.1.call-start = ((), (), s32[]{:S(2)}) async-start(), calls=%async_computation.5 | async-start | bytes 4718592 | tf_op jit(solution)/shard_map/reduce_scatter | solution.py:52
Sparse Core Ops, SparseCore 0:
  9.6 84.7 all-gather.8
  183.4 148.9 reduce-scatter.2
  334.4 290.6 all-gather.4
  683.0 106.0 all-gather.6
  791.9 49.9 reduce-scatter.4
where the time goes:
time: 850 us
  waiting for transfers between devices  559 us (66%)
  blocking collectives  141 us (17%)
  matrix products  90.6 us (11%)
  other arithmetic  34.9 us (4%)
  between operations  16.3 us (2%)
    all_gather x1, waiting for transfers between devices, per_device(): full_head = lax.all_gather(student_head, 'teacher', axis=0, tiled=True)  288 us
    reduce_scatter x1, waiting for transfers between devices, per_device(): lax.psum_scatter(weighted, 'teacher', scatter_dimension=0, tiled=True)  137 us
    all_gather x1, waiting for transfers between devices, per_device(): lax.all_gather(teacher_hidden[0], 'vocab', axis=0, tiled=True)  86.4 us
    dot_general x1, matrix products, per_device(): jnp.dot(lax.all_gather(teacher_hidden[0], 'vocab', axis=0, tiled=True), h...  41.8 us
    psum x1, blocking collectives, per_device(): loss = lax.psum(partial_kl, ('teacher', 'vocab')) / TOK  40 us
    reduce_scatter x1, waiting for transfers between devices, per_device(): lax.psum_scatter(lax.dot_general(full_head, gradl, (((1,), (1,)), ((), ()...  37 us
    all_to_all x1, blocking collectives, per_device(): lax.all_to_all(student_hidden, 'teacher', split_axis=1, concat_axis=0, ti...  32.7 us
    dot_general x1, matrix products, per_device(): lax.dot_general(full_head, gradl, (((1,), (1,)), ((), ())), preferred_ele...  18.8 us
  transfers between devices with their start and end apart: 5, of which 5 were waited for; matrix products, arithmetic and copies ran while one was open for 5% of the time, Pallas kernels for 0%

commit v1 on v0

--- a/solution.py
+++ b/solution.py
@@ -4,6 +4,17 @@
 from jax.sharding import PartitionSpec as P
 
 TOK = 1024
+
+
+def set_the_spots(block_here, which_dim):
+    block_here = jnp.moveaxis(block_here, 0, which_dim)
+    all_values = block_here.shape
+    oldest = block_here.reshape(
+        *all_values[:which_dim],
+        all_values[which_dim] * all_values[which_dim + 1],
+        *all_values[which_dim + 2 :]
+    )
+    return oldest
 
 
 def teacher_stats(logits):
@@ -40,7 +51,27 @@
         lax.psum_scatter(confid, "teacher", scatter_dimension=0, tiled=True),
     )
     raw = wsum / csum[:, None]
-    full_head = lax.all_gather(student_head, "teacher", axis=0, tiled=True)
+
+    def report_slots_on_mesh(mine, lane_axis, join_dim):
+        num = jax.lax.axis_size(lane_axis)
+        views = [(m, (m + 1) % num) for m in range(num)]
+        mid_arr, g_now = ([], [])
+        grid = [(nth, it) for it, nth in views]
+        for dd in range(num - 1):
+            if dd % 2 == 0:
+                y_new = jax.lax.ppermute(mid_arr[-1] if mid_arr else mine, lane_axis, perm=views)
+                mid_arr.append(y_new)
+            else:
+                g_now.append(jax.lax.ppermute(g_now[-1] if g_now else mine, lane_axis, grid))
+        field_out = jnp.stack([*mid_arr[::-1], mine, *g_now])
+        k_now = len(mid_arr)
+        small = jax.lax.axis_index(lane_axis)
+        r1 = small - k_now
+        field_out = field_out[(jnp.arange(num) - r1) % num]
+        carry = set_the_spots(field_out, join_dim)
+        return carry
+
+    full_head = report_slots_on_mesh(student_head, "teacher", 0)
     slog = jnp.dot(student_hidden, full_head, preferred_element_type=jnp.float32)
     both_lse = paired_lse(jnp.stack([raw, slog]))
     target = raw - both_lse[0][:, None]

time: 850 us -> 1230 us (1.45)
  blocking collectives: 141 us -> 473 us
  local copies, waits for them, and re-layouts: 7.62 us -> 126 us
  waiting for transfers between devices: 559 us -> 455 us
  other arithmetic: 34.9 us -> 57 us
    unnamed x1, blocking collectives: 10.4 us -> 351 us
    ppermute x0 -> x3, waiting for transfers between devices: none -> 309 us  [the longest x2 309 us: report_slots_on_mesh(): jax.lax.ppermute(mid_arr[-1] if mid_arr else mine, lane_axis, perm=views)]
    all_gather x1 -> x0, waiting for transfers between devices: 288 us -> none  [per_device(): full_head = lax.all_gather(student_head, 'teacher', axis=0, tiled=True)]
    reduce_scatter x1, waiting for transfers between devices: 137 us -> 0.01 us  [per_device(): lax.psum_scatter(weighted, 'teacher', scatter_dimension=0, tiled=True)]
    unnamed x11 -> x30, local copies, waits for them, and re-layouts: 5.11 us -> 72.1 us
    gather x0 -> x6, local copies, waits for them, and re-layouts: none -> 51 us  [report_slots_on_mesh(): field_out = field_out[(jnp.arange(num) - r1) % num]]
    all_gather x1, waiting for transfers between devices: 9.04 us -> 57.9 us  [per_device(): all_grads = lax.all_gather(gradl, 'teacher', axis=0, tiled=True)]
    reduce_scatter x1, waiting for transfers between devices: 37 us -> 0.02 us  [per_device(): lax.psum_scatter(lax.dot_general(full_head, gradl, (((1,), (1,)), ((), ()...]
  transfers between devices with their start and end apart: 5 -> 7, of which waited for: 5 -> 3; matrix products, arithmetic and copies ran while one was open for 5% -> 14% of each run, Pallas kernels for 0% -> 0%
where the time goes in v1:
time: 1230 us; the launch traced here: 1220 us
  blocking collectives  473 us (38%)
  waiting for transfers between devices  455 us (37%)
  local copies, waits for them, and re-layouts  126 us (10%)
  matrix products  93.1 us (8%)
  other arithmetic  57 us (5%)
  between operations  16.3 us (1%)
    unnamed x1, blocking collectives  351 us
    ppermute x2, waiting for transfers between devices, report_slots_on_mesh(): jax.lax.ppermute(mid_arr[-1] if mid_arr else mine, lane_axis, perm=views)  309 us
    all_gather x1, waiting for transfers between devices, per_device(): lax.all_gather(teacher_hidden[0], 'vocab', axis=0, tiled=True)  86.4 us
    unnamed x30, local copies, waits for them, and re-layouts  72.1 us
    all_gather x1, waiting for transfers between devices, per_device(): all_grads = lax.all_gather(gradl, 'teacher', axis=0, tiled=True)  57.9 us
    gather x6, local copies, waits for them, and re-layouts, report_slots_on_mesh(): field_out = field_out[(jnp.arange(num) - r1) % num]  51 us
    dot_general x1, matrix products, per_device(): jnp.dot(lax.all_gather(teacher_hidden[0], 'vocab', axis=0, tiled=True), h...  41.8 us
    psum x1, blocking collectives, per_device(): loss = lax.psum(partial_kl, ('teacher', 'vocab')) / TOK  37.6 us
  transfers between devices with their start and end apart: 7, of which 3 were waited for; matrix products, arithmetic and copies ran while one was open for 14% of the time, Pallas kernels for 0%

profile of v1, /device:TPU:0, one launch (start us, length us, event | category | flops | bytes accessed | tf_op | source)
XLA Modules:
  0.0 1223.9 jit_solution(12021307973292721627)
XLA Ops:
  7.9 86.4 %all-gather.6.cloned.1.call-done = bf16[1,1024,4096]{2,1,0:T(8,128)(2,1)} async-done(((bf16[1,128,4096]{2,1,0:T(8,128)(2,1)}), bf16[1,1024,4096]{2,1,0:T(8,128)(2,1)}) %all-gather.6.cloned.1.call-update) | async-done | bytes 8388624 | tf_op jit(solution)/shard_map/all_gather | solution.py:40
  94.4 41.8 %fusion.10 = (f32[1024]{0:T(1024)S(1)}, f32[1024,4000]{0,1:T(8,128)}) fusion(bf16[1,4096,4000]{1,2,0:T(8,128)(2,1)} %param.5, bf16[1,1024,4096]{2,1,0:T(8,128)(2,1)} %all-gather.6.cloned.1.call-done), kind=kOutput, calls=%fused_computation.40 | convolution fusion | flops 33558528000 | bytes 57544704 | tf_op jit(solution)/shard_map/dot_general | solution.py:39
  136.2 14.0 %pmax.14 = f32[1024]{0:T(1024)S(1)} all-reduce(f32[1024]{0:T(1024)S(1)} %get-tuple-element.29), channel_id=1, replica_groups=mesh['teacher'=4,'vocab'=8] {'vocab'}, use_global_device_ids=true, to_apply=%region_1.0 | all-reduce | flops 1024 | bytes 8192 | tf_op jit(solution)/shard_map/pmax | solution.py:22
  150.2 7.6 multiply_reduce_fusion
  157.8 13.9 %all-reduce.1 = (f32[1024]{0:T(1024)S(1)}, f32[1024]{0:T(1024)S(1)}) all-reduce(f32[1024]{0:T(1024)S(1)} %get-tuple-element.16, f32[1024]{0:T(1024)S(1)} %get-tuple-element.15), channel_id=1, replica_groups=mesh['teacher'=4,'vocab'=8] {'vocab'}, use_global_device_ids=true, to_apply=%region_3.0 | all-reduce | flops 2048 | bytes 16384 | tf_op jit(solution)/shard_map/psum | solution.py:24
  171.7 11.5 subtract_multiply_fusion
  186.3 309.1 %collective-permute-done = bf16[1024,4000]{0,1:T(8,128)(2,1)} collective-permute-done((bf16[1024,4000]{0,1:T(8,128)(2,1)}, bf16[1024,4000]{0,1:T(8,128)(2,1)}, u32[]{:S(2)}, u32[]{:S(2)}) %collective-permute-start) | collective-permute-done | bytes 8192032 | tf_op jit(solution)/shard_map/ppermute | solution.py:62
  497.5 351.2 %all-reduce = f32[1024]{0:T(1024)S(1)} all-reduce(f32[1024]{0:T(1024)S(1)} %get-tuple-element.25), channel_id=4, replica_groups=mesh['teacher'=4,'vocab'=8] {'teacher'}, use_global_device_ids=true, to_apply=%region_7.0.clone | all-reduce | flops 1024 | bytes 8192
  850.8 2.6 gather_fusion.4
  853.4 23.1 %pad_maximum_fusion = bf16[4,1024,4000]{1,2,0:T(8,128)(2,1)} fusion(bf16[1,1024,4000]{1,2,0:T(8,128)(2,1)} %bitcast.6, bf16[1,1024,4000]{1,2,0:T(8,128)(2,1)} %bitcast.47, bf16[1,1024,4000]{1,2,0:T(8,128)(2,1)} %bitcast.4, bf16[1,1024,4000]{1,2,0:T(8,128)(2,1)} %bitcast.3), kind=kLoop, calls=%fused_computation.5 | loop fusion | flops 49152000 | bytes 65536000 | tf_op jit(solution)/shard_map/stack | solution.py:66
  876.4 20.1 %fusion.8 = (bf16[4,1024,896]{1,2,0:T(8,128)(2,1)}, bf16[4,1024,896]{1,2,0:T(8,128)(2,1)}, bf16[4,1024,896]{1,2,0:T(8,128)(2,1)}, bf16[4,1024,896]{1,2,0:T(8,128)(2,1)}) fusion(bf16[4,1024,4000]{1,2,0:T(8,128)(2,1)} %pad_maximum_fusion), kind=kLoop, calls=%fused_computation.38 | loop fusion | bytes 58720256 | tf_op jit(solution)/shard_map/gather | solution.py:70
  896.5 7.1 gather_fusion.3
  903.6 7.1 gather_fusion.2
  910.7 7.0 gather_fusion.1
  917.8 7.1 gather_fusion
  924.8 7.1 constant_dynamic-update-slice_fusion.4
  932.0 3.9 constant_dynamic-update-slice_fusion.3
  935.9 7.1 constant_dynamic-update-slice_fusion.2
  943.0 3.9 constant_dynamic-update-slice_fusion.1
  948.9 39.8 %copy.14 = bf16[4,1024,4000]{2,1,0:T(8,128)(2,1)} copy(bf16[4,1024,4000]{1,2,0:T(8,128)(2,1)} %constant_dynamic-update-slice_fusion) | data formatting | bytes 65536000
  988.8 17.6 %fusion.11 = f32[4000,256]{1,0:T(8,128)} fusion(bf16[4096,4000]{1,0:T(8,128)(2,1)} %bitcast.44, bf16[256,4096]{1,0:T(8,128)(2,1)S(1)} %copy-done.5), kind=kOutput, calls=%fused_computation.41 | convolution fusion | flops 8388608000 | bytes 38961152 | tf_op jit(solution)/shard_map/dot_general | solution.py:75
  1006.5 2.6 fusion.7
  1011.6 13.6 %pmax.15 = f32[2,256]{1,0:T(2,128)S(1)} all-reduce(f32[2,256]{1,0:T(2,128)S(1)} %fusion.4), channel_id=1, replica_groups=mesh['teacher'=4,'vocab'=8] {'vocab'}, use_global_device_ids=true, to_apply=%region_9.10 | all-reduce | flops 512 | bytes 4096 | tf_op jit(solution)/shard_map/pmax | solution.py:32
  1025.2 4.0 exponential_reduce_fusion
  1029.2 13.9 %psum.30 = f32[2,256]{1,0:T(2,128)S(1)} all-reduce(f32[2,256]{1,0:T(2,128)S(1)} %exponential_reduce_fusion), channel_id=1, replica_groups=mesh['teacher'=4,'vocab'=8] {'vocab'}, use_global_device_ids=true, to_apply=%region_11.12 | all-reduce | flops 512 | bytes 4096 | tf_op jit(solution)/shard_map/psum | solution.py:33
  1043.0 5.6 subtract_convert_fusion
  1048.6 17.8 %fusion.12 = f32[4096,256]{1,0:T(8,128)} fusion(bf16[4096,4000]{1,0:T(8,128)(2,1)} %bitcast.45, bf16[256,4000]{0,1:T(8,128)(2,1)S(1)} %get-tuple-element.23), kind=kOutput, calls=%fused_computation.42 | convolution fusion | flops 8388608000 | bytes 39010304 | tf_op jit(solution)/shard_map/dot_general | solution.py:84
  1070.6 29.0 %all_to_all.19 = bf16[256,4,1024]{0,2,1:T(8,128)(2,1)S(1)} all-to-all(bf16[256,4,1024]{0,2,1:T(8,128)(2,1)} %bitcast.51), channel_id=1, replica_groups=mesh['teacher'=4,'vocab'=8] {'teacher'}, dimensions={1} | all-to-all | bytes 4194304 | tf_op jit(solution)/shard_map/all_to_all | solution.py:91
  1099.6 2.5 copy.16
  1102.1 37.6 %psum.31 = f32[]{:T(128)} all-reduce(f32[]{:T(128)} %get-tuple-element.24), channel_id=1, replica_groups=mesh['teacher'=4,'vocab'=8] {'teacher','vocab'}, use_global_device_ids=true, to_apply=%region_13.14 | all-reduce | flops 1 | bytes 8 | tf_op jit(solution)/shard_map/psum | solution.py:81
  1142.5 57.9 %all-gather.4.cloned.1.call-done = bf16[1024,4000]{0,1:T(8,128)(2,1)} async-done(((bf16[256,4000]{0,1:T(8,128)(2,1)}), bf16[1024,4000]{0,1:T(8,128)(2,1)}) %all-gather.4.cloned.1.call-update) | async-done | bytes 8192016 | tf_op jit(solution)/shard_map/all_gather | solution.py:92
  1200.4 15.9 %convolution_bitcast_fusion = f32[1024,4000]{0,1:T(8,128)} fusion(bf16[1024,4000]{0,1:T(8,128)(2,1)} %all-gather.4.cloned.1.call-done, bf16[1024,1024]{1,0:T(8,128)(2,1)} %bitcast.52), kind=kOutput, calls=%fused_computation.12 | convolution fusion | flops 8388608000 | bytes 26673152 | tf_op jit(solution)/shard_map/dot_general | solution.py:93
  (48 shorter events, 18.1 us)
Async XLA Ops:
  7.2 87.2 %all-gather.6.cloned.1.call-start = ((), (), s32[]{:S(2)}) async-start(), calls=%async_computation.6 | async-start | bytes 9437184 | tf_op jit(solution)/shard_map/all_gather | solution.py:40
  7.9 998.6 %reduce-scatter.3.cloned.1.call-start = ((), (), s32[]{:S(2)}) async-start(), calls=%async_computation.3 | async-start | bytes 20480000 | tf_op jit(solution)/shard_map/reduce_scatter | solution.py:50
  183.2 313.0 %copy-start.7 = (u32[32]{0:T(128)S(1)}, u32[32]{0:T(128)}, u32[]{:S(2)}) copy-start(u32[32]{0:T(128)} %constant.36) | copy-start | bytes 388
  183.3 957.2 %reduce-scatter.5.cloned.1.call-start = ((), (), s32[]{:S(2)}) async-start(), calls=%async_computation.4 | async-start | bytes 4718592 | tf_op jit(solution)/shard_map/reduce_scatter | solution.py:83
  183.3 312.1 %collective-permute-start = (bf16[1024,4000]{0,1:T(8,128)(2,1)}, bf16[1024,4000]{0,1:T(8,128)(2,1)}, u32[]{:S(2)}, u32[]{:S(2)}) collective-permute-start(bf16[1024,4000]{0,1:T(8,128)(2,1)} %param.7), channel_id=1, source_target_pairs={{0,8},{8,16},{16,24},{24,0},{1,9},{9,17},{17,25},{25,1},{2,10},{10... | collective-permute-start | bytes 24576008 | tf_op jit(solution)/shard_map/ppermute | solution.py:62
  185.1 663.7 %collective-permute-start.2 = (bf16[1024,4000]{0,1:T(8,128)(2,1)}, bf16[1024,4000]{0,1:T(8,128)(2,1)}, u32[]{:S(2)}, u32[]{:S(2)}) collective-permute-start(bf16[1024,4000]{0,1:T(8,128)(2,1)} %param.7), channel_id=1, source_target_pairs={{8,0},{16,8},{24,16},{0,24},{9,1},{17,9},{25,17},{1,25},{10,2},{18... | collective-permute-start | bytes 24576008 | tf_op jit(solution)/shard_map/ppermute | solution.py:65
  495.4 353.3 %collective-permute-start.1 = (bf16[1024,4000]{0,1:T(8,128)(2,1)}, bf16[1024,4000]{0,1:T(8,128)(2,1)}, u32[]{:S(2)}, u32[]{:S(2)}) collective-permute-start(bf16[1024,4000]{0,1:T(8,128)(2,1)} %collective-permute-done), channel_id=1, source_target_pairs={{0,8},{8,16},{16,24},{24,0},{1,9},{9,17},{17,25},{25,1},{2,10},{10... | collective-permute-start | bytes 24576008 | tf_op jit(solution)/shard_map/ppermute | solution.py:62
  924.8 7.1 copy-start.2
  932.0 11.0 slice-start
  935.9 7.1 slice-start.1
  943.0 3.9 copy-start.3
  948.9 39.9 %copy-start.5 = (bf16[256,4096]{1,0:T(8,128)(2,1)S(1)}, bf16[256,4096]{1,0:T(8,128)(2,1)}, u32[]{:S(2)}) copy-start(bf16[256,4096]{1,0:T(8,128)(2,1)} %param.6) | copy-start | bytes 6291460
  1006.5 4.6 copy-start.1
  1009.1 2.0 copy-start
  1048.6 17.8 %copy-start.4 = (bf16[256,4000]{0,1:T(8,128)(2,1)}, bf16[256,4000]{0,1:T(8,128)(2,1)S(1)}, u32[]{:S(2)}) copy-start(bf16[256,4000]{0,1:T(8,128)(2,1)S(1)} %get-tuple-element.23) | copy-start | bytes 6144004
  1066.5 1.6 copy-start.6
  1066.5 133.9 %all-gather.4.cloned.1.call-start = ((), (), s32[]{:S(2)}) async-start(), calls=%async_computation.5 | async-start | bytes 10240000 | tf_op jit(solution)/shard_map/all_gather | solution.py:92
Sparse Core Ops, SparseCore 0:
  9.6 84.7 all-gather.5
  183.4 281.6 reduce-scatter.2
  1066.6 47.2 reduce-scatter.4
  1115.7 84.6 all-gather.3
